TPU v7x, 32 devices: a whole 2x2x4 slice. The times are simulated.
32 devices in a mesh: groups: 2 (over y), qry: 4 (over x, core), ref: 4 (over z).
Axes of the slice: x: 2, y: 2, z: 4, core: 2. Of those that a mesh axis runs over, the one named last changes fastest.
Arguments:
- query_feats: bfloat16 [1024, 9, 3840], P(('groups', 'qry')), parts along dimension 0, may hold values from -6 to 6
- ref_feats: bfloat16 [256, 4, 9, 3840], P(('groups', 'ref'), 'qry'), parts along dimension 0, may hold values from -6 to 6
- pair_table: int32 [8, 4], P('groups'), parts along dimension 0, may hold values from 0 to 1, as said below
- lengths: int32 [4], P('groups'), parts along dimension 0, may hold values from 1 to 96, 128 in all
- query_len: int32 [2], P('groups'), parts along dimension 0, may hold values from 64 to 128
- conv1_weight: float32 [3, 3, 32], replicated, may hold values from -2 to 2
- conv1_bias: float32 [32], replicated, may hold values from -3 to 3
- conv2_weight: bfloat16 [3, 3, 64, 32], replicated, may hold values from -0.375 to 0.375
- conv2_bias: float32 [64], replicated, may hold values from -3 to 3
- conv3_weight: bfloat16 [3, 3, 128, 64], replicated, may hold values from -0.25 to 0.25
- conv3_bias: float32 [128], replicated, may hold values from -3 to 3
- conv4_weight: bfloat16 [128], replicated, may hold values from -0.5 to 0.5
- conv4_bias: float32 [1], replicated, may hold values from -3 to 3
Outputs:
- score_map: float32 [256, 128], P(('groups', 'qry'), 'ref'), parts along dimension 0
- video_scores: float32 [4], P('groups'), parts along dimension 0
There are 2 independent parts, one for each index of `groups`. A program takes and returns all parts, laid end to end along the dimension named above; an argument that names none is the same for every part. Nothing has to cross between parts.
Inputs may be any that keep to these rules, and one draw needn't show every extreme that they name: `pair_table`: in each row, at most 1 of the 1 tiles in the block of one index of ref are 1, and some such block holds exactly 1 in every draw.
All inputs are finite; a program needn't handle non-finite values.
Results may differ from a plain program's by a relative error of at most 0.01.
Values may be sent and summed in bfloat16 or wider, within the bound.
No kernel may reach another device: no remote copies, remote signals or barrier semaphores. Data moves between devices by JAX's collectives and lax.ppermute only.
A program may use at most 128 MiB of HBM per device.

v0:
```python
import math

import jax
import jax.numpy as jnp
from jax import lax
from jax.sharding import PartitionSpec as P

MOST = 1


def padded_2(block, sides, width):
    for axis, dim in sides:
        count = lax.axis_size(axis)
        forward = [(i, i + 1) for i in range(count - 1)]
        backward = [(target, source) for source, target in forward]
        low = lax.ppermute(
            lax.slice_in_dim(block, block.shape[dim] - width, None, axis=dim), axis, forward
        )
        high = lax.ppermute(lax.slice_in_dim(block, 0, width, axis=dim), axis, backward)
        block = jnp.concatenate([low, block, high], axis=dim)
    return block


def slot_table(mask, most):
    width = mask.shape[-1]
    ranking = jnp.cumsum(mask, axis=-1) - 1
    slot_ids = jnp.arange(most, dtype=jnp.int32)
    chosen = (mask[..., None, :] == 1) & (ranking[..., None, :] == slot_ids[:, None])
    picked = jnp.sum(jnp.where(chosen, jnp.arange(width, dtype=jnp.int32), 0), axis=-1)
    return (chosen, picked)


def frame_sims(query_mat, ref_mat, regions):
    products = lax.dot_general(
        query_mat, ref_mat, (((1,), (1,)), ((), ())), preferred_element_type=jnp.float32
    )
    frames = query_mat.shape[0] // regions
    others = ref_mat.shape[0] // regions
    best = jnp.max(products.reshape(frames, regions, others, regions), axis=3)
    return jnp.sum(best, axis=1) * (1.0 / (regions * math.sqrt(query_mat.shape[1])))


def conv_layer(padded, weights, bias, block_rows, use_pool):
    channels = padded.shape[0]
    height = padded.shape[1] - 2
    width = padded.shape[2] - 2
    block_rows = math.gcd(height, block_rows)
    outputs = weights.shape[0]
    accuracy = lax.Precision.HIGHEST if padded.dtype == jnp.float32 else None

    def one_block(position):
        window = lax.dynamic_slice_in_dim(padded, position * block_rows, block_rows + 2, 1)
        stacked = jnp.concatenate(
            [
                window[:, shift_row : shift_row + block_rows, shift_col : shift_col + width]
                for shift_row in range(3)
                for shift_col in range(3)
            ],
            axis=0,
        )
        result = jnp.dot(
            weights,
            stacked.reshape(9 * channels, block_rows * width),
            preferred_element_type=jnp.float32,
            precision=accuracy,
        )
        result = (result + bias[:, None]).reshape(outputs, block_rows, width)
        result = jnp.maximum(result, 0.0)
        if use_pool:
            result = jnp.max(
                result.reshape(outputs, block_rows // 2, 2, width // 2, 2), axis=(2, 4)
            )
        return result

    blocks = lax.map(one_block, jnp.arange(height // block_rows, dtype=jnp.int32))
    return jnp.transpose(blocks, (1, 0, 2, 3)).reshape(outputs, -1, blocks.shape[-1])


def weight_matrix(weight):
    return jnp.transpose(weight, (2, 0, 1, 3)).reshape(weight.shape[2], -1)


def body(
    query_feats,
    ref_feats,
    pair_table,
    lengths,
    query_len,
    conv1_weight,
    conv1_bias,
    conv2_weight,
    conv2_bias,
    conv3_weight,
    conv3_bias,
    conv4_weight,
    conv4_bias,
):
    qry_index = lax.axis_index("qry")
    ref_index = lax.axis_index("ref")
    frames = query_feats.shape[0]
    regions = query_feats.shape[1]
    channels = query_feats.shape[2]
    tiles_here = pair_table.shape[1] // lax.axis_size("ref")
    tile_rows = ref_feats.shape[0] // tiles_here
    query_mat = query_feats.reshape(frames * regions, channels)
    own_mask = lax.dynamic_slice(pair_table, (qry_index, ref_index * tiles_here), (1, tiles_here))[
        0
    ]
    chosen, picked = slot_table(own_mask, MOST)
    shards = lax.all_gather(ref_feats, "qry", axis=1, tiled=True)
    senders = shards.shape[1]
    sims = frame_sims(query_mat, shards.reshape(tile_rows * senders * regions, channels), regions)
    sims = sims.reshape(1, frames, tile_rows, senders)
    tile_sims = sims.reshape(MOST, frames, frames)
    placed = jnp.einsum(
        "st,sqf->qtf", chosen.astype(jnp.float32), tile_sims, precision=lax.Precision.HIGHEST
    )
    sim_map = placed.reshape(frames, tiles_here * frames)
    padded = padded_2(sim_map, (("qry", 0), ("ref", 1)), 1)
    first_weights = jnp.transpose(conv1_weight, (2, 0, 1)).reshape(conv1_weight.shape[2], 9)
    first = conv_layer(padded[None], first_weights, conv1_bias, 32, True).astype(jnp.bfloat16)
    padded = padded_2(first, (("qry", 1), ("ref", 2)), 1)
    second = conv_layer(padded, weight_matrix(conv2_weight), conv2_bias, 16, True).astype(
        jnp.bfloat16
    )
    padded = padded_2(second, (("qry", 1), ("ref", 2)), 1)
    third = conv_layer(padded, weight_matrix(conv3_weight), conv3_bias, 16, False).astype(
        jnp.bfloat16
    )
    map_rows = third.shape[1]
    map_cols = third.shape[2]
    score_map = (
        jnp.dot(
            conv4_weight[None],
            third.reshape(third.shape[0], -1),
            preferred_element_type=jnp.float32,
        ).reshape(map_rows, map_cols)
        + conv4_bias[0]
    )
    ends = jnp.cumsum(lengths)
    starts = ends - lengths
    column = ref_index * map_cols + jnp.arange(map_cols, dtype=jnp.int32)
    member = (column[:, None] >= starts[None, :]) & (column[:, None] < ends[None, :])
    peaks = jnp.max(jnp.where(member[None], score_map[:, :, None], -jnp.inf), axis=1)
    peaks = lax.pmax(peaks, "ref")
    row_ids = qry_index * map_rows + jnp.arange(map_rows, dtype=jnp.int32)
    partial_value = jnp.sum(jnp.where((row_ids < query_len[0])[:, None], peaks, 0.0), axis=0)
    totals = lax.psum(partial_value, "qry")
    return (score_map, totals / query_len[0].astype(jnp.float32))


def solution(mesh):
    placed = (
        P(("groups", "qry"), None, None),
        P(("groups", "ref"), "qry", None, None),
        P("groups", None),
        P("groups"),
        P("groups"),
        P(),
        P(),
        P(),
        P(),
        P(),
        P(),
        P(),
        P(),
    )
    return jax.shard_map(
        body,
        mesh=mesh,
        in_specs=placed,
        out_specs=(P(("groups", "qry"), "ref"), P("groups")),
        check_vma=False,
    )
```

profile of v0, /device:TPU:0, one launch (start us, length us, event | category | flops | bytes accessed | tf_op | source)
XLA Modules:
  0.0 248.4 jit_solution(3101193552977106752)
XLA Ops:
  10.5 62.7 %all-gather.2.cloned.1.call-done = bf16[32,4,9,3840]{3,0,2,1:T(8,128)(2,1)} async-done(((bf16[32,1,9,3840]{3,0,2,1:T(8,128)(2,1)}), bf16[32,4,9,3840]{3,0,2,1:T(8,128)(2,1)}) %all-gather.2.cloned.1.call-update) | async-done | bytes 8847376 | tf_op jit(solution)/shard_map/all_gather | solution.py:110
  73.2 8.6 %copy.62 = bf16[32,4,9,3840]{3,1,0,2:T(4,128)(2,1)} copy(bf16[32,4,9,3840]{3,0,2,1:T(8,128)(2,1)} %all-gather.2.cloned.1.call-done) | data formatting | bytes 17694720 | tf_op jit(solution)/shard_map/all_gather | solution.py:110
  81.8 12.7 %reshape.195 = bf16[128,9,3840,1]{2,0,1,3:T(8,128)(2,1)} reshape(bf16[32,4,9,3840]{3,1,0,2:T(4,128)(2,1)} %copy.62) | data formatting | bytes 17694720 | tf_op jit(solution)/shard_map/dot_general | solution.py:34
  94.5 18.8 %fusion.7 = f32[128,9,128]{2,0,1:T(8,128)S(1)} fusion(bf16[128,9,3840,1]{2,0,1,3:T(8,128)(2,1)} %reshape.195, bf16[128,9,3840]{2,0,1:T(8,128)(2,1)} %param.19), kind=kOutput, calls=%fused_computation.40 | convolution fusion | flops 10193338368 | bytes 18284544 | tf_op jit(solution)/shard_map/dot_general | solution.py:34
  118.7 3.4 %collective-permute-start.2 = (f32[130,1]{1,0:T(8,128)S(1)}, f32[130,1]{1,0:T(8,128)S(1)}, u32[]{:S(2)}, u32[]{:S(2)}) collective-permute-start(f32[130,1]{1,0:T(8,128)S(1)} %get-tuple-element.223), channel_id=1, source_target_pairs={{0,1},{1,2},{2,3},{4,5},{5,6},{6,7},{8,9},{9,10},{10,11},{12,13},{... | collective-permute-start | bytes 1568 | tf_op jit(solution)/shard_map/ppermute | solution.py:16
  124.1 4.3 %collective-permute-done.3 = f32[130,1]{1,0:T(8,128)S(1)} collective-permute-done((f32[130,1]{1,0:T(8,128)S(1)}, f32[130,1]{1,0:T(8,128)S(1)}, u32[]{:S(2)}, u32[]{:S(2)}) %collective-permute-start.3) | collective-permute-done | bytes 552 | tf_op jit(solution)/shard_map/ppermute | solution.py:19
  128.5 23.2 %while.30 = (s32[]{:T(128)}, bf16[4,32,16,64]{3,2,0,1:T(8,128)(2,1)S(1)}, s32[4]{0:T(128)S(1)}, f32[1,130,130]{2,1,0:T(8,128)S(1)}, f32[32,9]{0,1:T(8,128)S(1)},...) while((s32[]{:T(128)}, ...), condition=%wide.region_4.5_spmd, body=%wide.region_2.4_spmd.sunk | while | flops 14647306 | bytes 2885173 | solution.py:75
  131.6 2.5 %reduce_max.42 = bf16[32,16,64]{0,2,1:T(8,128)(2,1)S(1)} reduce(bf16[32,16,2,64,2]{0,4,3,2,1:T(2,128)(2,1)S(1)} %bitcast.115, bf16[]{:T(256)} %constant.179..sunk), dimensions={2,4}, to_apply=%region_3.3 | reduce | flops 98304 | bytes 327682 | tf_op jit(solution)/shard_map/while/body/eval_jaxpr/reduce_max | solution.py:70
  137.4 2.5 %reduce_max.42 = bf16[32,16,64]{0,2,1:T(8,128)(2,1)S(1)} reduce(bf16[32,16,2,64,2]{0,4,3,2,1:T(2,128)(2,1)S(1)} %bitcast.115, bf16[]{:T(256)} %constant.179..sunk), dimensions={2,4}, to_apply=%region_3.3 | reduce | flops 98304 | bytes 327682 | tf_op jit(solution)/shard_map/while/body/eval_jaxpr/reduce_max | solution.py:70
  143.2 2.5 %reduce_max.42 = bf16[32,16,64]{0,2,1:T(8,128)(2,1)S(1)} reduce(bf16[32,16,2,64,2]{0,4,3,2,1:T(2,128)(2,1)S(1)} %bitcast.115, bf16[]{:T(256)} %constant.179..sunk), dimensions={2,4}, to_apply=%region_3.3 | reduce | flops 98304 | bytes 327682 | tf_op jit(solution)/shard_map/while/body/eval_jaxpr/reduce_max | solution.py:70
  149.0 2.5 %reduce_max.42 = bf16[32,16,64]{0,2,1:T(8,128)(2,1)S(1)} reduce(bf16[32,16,2,64,2]{0,4,3,2,1:T(2,128)(2,1)S(1)} %bitcast.115, bf16[]{:T(256)} %constant.179..sunk), dimensions={2,4}, to_apply=%region_3.3 | reduce | flops 98304 | bytes 327682 | tf_op jit(solution)/shard_map/while/body/eval_jaxpr/reduce_max | solution.py:70
  151.7 2.7 %collective-permute-start.4 = (bf16[32,1,64]{2,1,0:T(2,128)(2,1)S(1)}, bf16[32,1,64]{2,1,0:T(2,128)(2,1)S(1)}, u32[]{:S(2)}, u32[]{:S(2)}) collective-permute-start(bf16[32,1,64]{2,1,0:T(2,128)(2,1)S(1)} %get-tuple-element.217), channel_id=1, source_target_pairs={{0,4},{4,8},{8,12},{1,5},{5,9},{9,13},{2,6},{6,10},{10,14},{3,7},{... | collective-permute-start | bytes 12296 | tf_op jit(solution)/shard_map/ppermute | solution.py:16
  155.8 2.7 %collective-permute-done.5 = bf16[32,1,64]{2,1,0:T(2,128)(2,1)S(1)} collective-permute-done((bf16[32,1,64]{2,1,0:T(2,128)(2,1)S(1)}, bf16[32,1,64]{2,1,0:T(2,128)(2,1)S(1)}, u32[]{:S(2)}, u32[]{:S(2)}) %collective-permute-start.5) | collective-permute-done | bytes 4128 | tf_op jit(solution)/shard_map/ppermute | solution.py:19
  159.3 3.4 %collective-permute-start.6 = (bf16[32,66,1]{1,0,2:T(8,128)(2,1)S(1)}, bf16[32,66,1]{1,0,2:T(8,128)(2,1)S(1)}, u32[]{:S(2)}, u32[]{:S(2)}) collective-permute-start(bf16[32,66,1]{1,0,2:T(8,128)(2,1)S(1)} %copy.64), channel_id=1, source_target_pairs={{0,1},{1,2},{2,3},{4,5},{5,6},{6,7},{8,9},{9,10},{10,11},{12,13},{... | collective-permute-start | bytes 12680 | tf_op jit(solution)/shard_map/ppermute | solution.py:16
  165.7 2.9 %collective-permute-done.7 = bf16[32,66,1]{1,0,2:T(8,128)(2,1)S(1)} collective-permute-done((bf16[32,66,1]{1,0,2:T(8,128)(2,1)S(1)}, bf16[32,66,1]{1,0,2:T(8,128)(2,1)S(1)}, u32[]{:S(2)}, u32[]{:S(2)}) %collective-permute-start.7) | collective-permute-done | bytes 4256 | tf_op jit(solution)/shard_map/ppermute | solution.py:19
  170.1 32.3 %while.31 = (s32[]{:T(128)}, bf16[4,64,8,32]{1,3,2,0:T(8,128)(2,1)}, s32[4]{0:T(128)S(1)}, bf16[32,66,66]{2,0,1:T(8,128)(2,1)S(1)}, bf16[64,288]{1,0:T(8,128)(2,...) while((s32[]{:T(128)}, ...), condition=%wide.region_7.8_spmd, body=%wide.region_5.7_spmd.sunk | while | flops 37994504 | bytes 4822013 | solution.py:75
  174.0 2.4 concatenate.35
  182.1 2.4 concatenate.35
  203.1 2.9 %collective-permute-start.8 = (bf16[64,1,32]{0,2,1:T(8,128)(2,1)S(1)}, bf16[64,1,32]{0,2,1:T(8,128)(2,1)S(1)}, u32[]{:S(2)}, u32[]{:S(2)}) collective-permute-start(bf16[64,1,32]{0,2,1:T(8,128)(2,1)S(1)} %get-tuple-element.221), channel_id=1, source_target_pairs={{0,4},{4,8},{8,12},{1,5},{5,9},{9,13},{2,6},{6,10},{10,14},{3,7},{... | collective-permute-start | bytes 12296 | tf_op jit(solution)/shard_map/ppermute | solution.py:16
  211.0 3.4 %collective-permute-start.10 = (bf16[64,34,1]{0,2,1:T(2,128)(2,1)S(1)}, bf16[64,34,1]{0,2,1:T(2,128)(2,1)S(1)}, u32[]{:S(2)}, u32[]{:S(2)}) collective-permute-start(bf16[64,34,1]{0,2,1:T(2,128)(2,1)S(1)} %get-tuple-element.219), channel_id=1, source_target_pairs={{0,1},{1,2},{2,3},{4,5},{5,6},{6,7},{8,9},{9,10},{10,11},{12,13},{... | collective-permute-start | bytes 13064 | tf_op jit(solution)/shard_map/ppermute | solution.py:16
  217.5 2.6 %collective-permute-done.11 = bf16[64,34,1]{0,2,1:T(2,128)(2,1)S(1)} collective-permute-done((bf16[64,34,1]{0,2,1:T(2,128)(2,1)S(1)}, bf16[64,34,1]{0,2,1:T(2,128)(2,1)S(1)}, u32[]{:S(2)}, u32[]{:S(2)}) %collective-permute-start.11) | collective-permute-done | bytes 4384 | tf_op jit(solution)/shard_map/ppermute | solution.py:19
  221.2 4.8 %while.32 = (s32[]{:T(128)}, bf16[2,128,16,32]{1,3,2,0:T(8,128)(2,1)S(1)}, s32[2]{0:T(128)S(1)}, bf16[64,34,34]{0,2,1:T(8,128)(2,1)S(1)}, bf16[128,576]{1,0:T(8,...) while((s32[]{:T(128)}, ...), condition=%wide.region_9.10_spmd, body=%wide.region_8.9_spmd.sunk | while | flops 75694088 | bytes 3490551 | solution.py:75
  226.6 8.5 %pmax.7 = f32[32,2]{0,1:T(2,128)S(1)} all-reduce(f32[32,2]{0,1:T(2,128)S(1)} %select_reduce_fusion), channel_id=1, replica_groups=mesh['groups'=2,'qry'=4,'ref'=4] {'ref'}, use_global_device_ids=true, to_apply=%region_12.13 | all-reduce | flops 64 | bytes 512 | tf_op jit(solution)/shard_map/pmax | solution.py:145
  235.2 5.8 %psum.7 = f32[2]{0:T(128)S(1)} all-reduce(f32[2]{0:T(128)S(1)} %select_reduce_fusion.1), channel_id=1, replica_groups=mesh['groups'=2,'qry'=4,'ref'=4] {'qry'}, use_global_device_ids=true, to_apply=%region_14.15 | all-reduce | flops 2 | bytes 16 | tf_op jit(solution)/shard_map/psum | solution.py:148
  (207 shorter events, 63.9 us)
Async XLA Ops:
  7.2 218.9 %copy-start = (bf16[128]{0:T(256)(128)(2,1)S(1)}, bf16[128]{0:T(256)(128)(2,1)}, u32[]{:S(2)}) copy-start(bf16[128]{0:T(256)(128)(2,1)} %param.30) | copy-start | bytes 772
  7.2 66.0 %all-gather.2.cloned.1.call-start = ((), (), s32[]{:S(2)}) async-start(), calls=%async_computation | async-start | bytes 11059200 | tf_op jit(solution)/shard_map/all_gather | solution.py:110
  94.5 28.9 %copy-start.6 = (f32[3,3,32]{2,1,0:T(4,128)S(1)}, f32[3,3,32]{2,1,0:T(4,128)}, u32[]{:S(2)}) copy-start(f32[3,3,32]{2,1,0:T(4,128)} %param.24) | copy-start | bytes 3460
  94.5 29.0 %copy-start.7 = (s32[2]{0:T(128)S(1)}, s32[2]{0:T(128)}, u32[]{:S(2)}) copy-start(s32[2]{0:T(128)} %param.22) | copy-start | bytes 28
  94.5 34.0 %copy-start.5 = (f32[32]{0:T(128)S(1)}, f32[32]{0:T(128)}, u32[]{:S(2)}) copy-start(f32[32]{0:T(128)} %param.25) | copy-start | bytes 388
  113.4 3.5 %collective-permute-start = (f32[1,128]{1,0:T(1,128)S(1)}, f32[1,128]{1,0:T(1,128)S(1)}, u32[]{:S(2)}, u32[]{:S(2)}) collective-permute-start(f32[1,128]{1,0:T(1,128)S(1)} %get-tuple-element.225), channel_id=1, source_target_pairs={{0,4},{4,8},{8,12},{1,5},{5,9},{9,13},{2,6},{6,10},{10,14},{3,7},{... | collective-permute-start | bytes 1544 | tf_op jit(solution)/shard_map/ppermute | solution.py:16
  115.6 3.1 %collective-permute-start.1 = (f32[1,128]{1,0:T(1,128)S(1)}, f32[1,128]{1,0:T(1,128)S(1)}, u32[]{:S(2)}, u32[]{:S(2)}) collective-permute-start(f32[1,128]{1,0:T(1,128)S(1)} %get-tuple-element.226), channel_id=1, source_target_pairs={{4,0},{8,4},{12,8},{5,1},{9,5},{13,9},{6,2},{10,6},{14,10},{7,3},{... | collective-permute-start | bytes 1544 | tf_op jit(solution)/shard_map/ppermute | solution.py:19
  118.7 5.3 %collective-permute-start.2 = (f32[130,1]{1,0:T(8,128)S(1)}, f32[130,1]{1,0:T(8,128)S(1)}, u32[]{:S(2)}, u32[]{:S(2)}) collective-permute-start(f32[130,1]{1,0:T(8,128)S(1)} %get-tuple-element.223), channel_id=1, source_target_pairs={{0,1},{1,2},{2,3},{4,5},{5,6},{6,7},{8,9},{9,10},{10,11},{12,13},{... | collective-permute-start | bytes 1568 | tf_op jit(solution)/shard_map/ppermute | solution.py:16
  122.1 6.2 %collective-permute-start.3 = (f32[130,1]{1,0:T(8,128)S(1)}, f32[130,1]{1,0:T(8,128)S(1)}, u32[]{:S(2)}, u32[]{:S(2)}) collective-permute-start(f32[130,1]{1,0:T(8,128)S(1)} %get-tuple-element.224), channel_id=1, source_target_pairs={{1,0},{2,1},{3,2},{5,4},{6,5},{7,6},{9,8},{10,9},{11,10},{13,12},{... | collective-permute-start | bytes 1568 | tf_op jit(solution)/shard_map/ppermute | solution.py:19
  128.5 36.1 %copy-start.1 = (bf16[3,3,64,32]{2,3,1,0:T(8,128)(2,1)S(1)}, bf16[3,3,64,32]{2,3,1,0:T(8,128)(2,1)}, u32[]{:S(2)}) copy-start(bf16[3,3,64,32]{2,3,1,0:T(8,128)(2,1)} %param.26) | copy-start | bytes 110596
  151.7 18.4 %copy-start.3 = (f32[64]{0:T(128)S(1)}, f32[64]{0:T(128)}, u32[]{:S(2)}) copy-start(f32[64]{0:T(128)} %param.27) | copy-start | bytes 772
  151.7 4.1 %collective-permute-start.4 = (bf16[32,1,64]{2,1,0:T(2,128)(2,1)S(1)}, bf16[32,1,64]{2,1,0:T(2,128)(2,1)S(1)}, u32[]{:S(2)}, u32[]{:S(2)}) collective-permute-start(bf16[32,1,64]{2,1,0:T(2,128)(2,1)S(1)} %get-tuple-element.217), channel_id=1, source_target_pairs={{0,4},{4,8},{8,12},{1,5},{5,9},{9,13},{2,6},{6,10},{10,14},{3,7},{... | collective-permute-start | bytes 12296 | tf_op jit(solution)/shard_map/ppermute | solution.py:16
  154.5 4.1 %collective-permute-start.5 = (bf16[32,1,64]{2,1,0:T(2,128)(2,1)S(1)}, bf16[32,1,64]{2,1,0:T(2,128)(2,1)S(1)}, u32[]{:S(2)}, u32[]{:S(2)}) collective-permute-start(bf16[32,1,64]{2,1,0:T(2,128)(2,1)S(1)} %get-tuple-element.218), channel_id=1, source_target_pairs={{4,0},{8,4},{12,8},{5,1},{9,5},{13,9},{6,2},{10,6},{14,10},{7,3},{... | collective-permute-start | bytes 12296 | tf_op jit(solution)/shard_map/ppermute | solution.py:19
  159.3 5.4 %collective-permute-start.6 = (bf16[32,66,1]{1,0,2:T(8,128)(2,1)S(1)}, bf16[32,66,1]{1,0,2:T(8,128)(2,1)S(1)}, u32[]{:S(2)}, u32[]{:S(2)}) collective-permute-start(bf16[32,66,1]{1,0,2:T(8,128)(2,1)S(1)} %copy.64), channel_id=1, source_target_pairs={{0,1},{1,2},{2,3},{4,5},{5,6},{6,7},{8,9},{9,10},{10,11},{12,13},{... | collective-permute-start | bytes 12680 | tf_op jit(solution)/shard_map/ppermute | solution.py:16
  163.1 5.5 %collective-permute-start.7 = (bf16[32,66,1]{1,0,2:T(8,128)(2,1)S(1)}, bf16[32,66,1]{1,0,2:T(8,128)(2,1)S(1)}, u32[]{:S(2)}, u32[]{:S(2)}) collective-permute-start(bf16[32,66,1]{1,0,2:T(8,128)(2,1)S(1)} %copy.65), channel_id=1, source_target_pairs={{1,0},{2,1},{3,2},{5,4},{6,5},{7,6},{9,8},{10,9},{11,10},{13,12},{... | collective-permute-start | bytes 12680 | tf_op jit(solution)/shard_map/ppermute | solution.py:19
  170.1 51.1 %copy-start.4 = (f32[128]{0:T(128)S(1)}, f32[128]{0:T(128)}, u32[]{:S(2)}) copy-start(f32[128]{0:T(128)} %param.29) | copy-start | bytes 1540
  203.1 5.0 %collective-permute-start.8 = (bf16[64,1,32]{0,2,1:T(8,128)(2,1)S(1)}, bf16[64,1,32]{0,2,1:T(8,128)(2,1)S(1)}, u32[]{:S(2)}, u32[]{:S(2)}) collective-permute-start(bf16[64,1,32]{0,2,1:T(8,128)(2,1)S(1)} %get-tuple-element.221), channel_id=1, source_target_pairs={{0,4},{4,8},{8,12},{1,5},{5,9},{9,13},{2,6},{6,10},{10,14},{3,7},{... | collective-permute-start | bytes 12296 | tf_op jit(solution)/shard_map/ppermute | solution.py:16
  206.1 4.0 %collective-permute-start.9 = (bf16[64,1,32]{0,2,1:T(8,128)(2,1)S(1)}, bf16[64,1,32]{0,2,1:T(8,128)(2,1)S(1)}, u32[]{:S(2)}, u32[]{:S(2)}) collective-permute-start(bf16[64,1,32]{0,2,1:T(8,128)(2,1)S(1)} %get-tuple-element.222), channel_id=1, source_target_pairs={{4,0},{8,4},{12,8},{5,1},{9,5},{13,9},{6,2},{10,6},{14,10},{7,3},{... | collective-permute-start | bytes 12296 | tf_op jit(solution)/shard_map/ppermute | solution.py:19
  211.0 6.5 %collective-permute-start.10 = (bf16[64,34,1]{0,2,1:T(2,128)(2,1)S(1)}, bf16[64,34,1]{0,2,1:T(2,128)(2,1)S(1)}, u32[]{:S(2)}, u32[]{:S(2)}) collective-permute-start(bf16[64,34,1]{0,2,1:T(2,128)(2,1)S(1)} %get-tuple-element.219), channel_id=1, source_target_pairs={{0,1},{1,2},{2,3},{4,5},{5,6},{6,7},{8,9},{9,10},{10,11},{12,13},{... | collective-permute-start | bytes 13064 | tf_op jit(solution)/shard_map/ppermute | solution.py:16
  214.4 5.6 %collective-permute-start.11 = (bf16[64,34,1]{0,2,1:T(2,128)(2,1)S(1)}, bf16[64,34,1]{0,2,1:T(2,128)(2,1)S(1)}, u32[]{:S(2)}, u32[]{:S(2)}) collective-permute-start(bf16[64,34,1]{0,2,1:T(2,128)(2,1)S(1)} %get-tuple-element.220), channel_id=1, source_target_pairs={{1,0},{2,1},{3,2},{5,4},{6,5},{7,6},{9,8},{10,9},{11,10},{13,12},{... | collective-permute-start | bytes 13064 | tf_op jit(solution)/shard_map/ppermute | solution.py:19
  226.5 15.1 %copy-start.2 = (f32[32,32]{1,0:T(8,128)}, f32[32,32]{1,0:T(8,128)S(1)}, u32[]{:S(2)}) copy-start(f32[32,32]{1,0:T(8,128)S(1)} %broadcast_add_fusion) | copy-start | bytes 12292
Sparse Core Ops, SparseCore 0:
  9.5 63.5 all-gather.1
where the time goes:
time: 250 us; the launch traced here: 248 us
  waiting for transfers between devices  80 us (32%)
  local copies, waits for them, and re-layouts  63.7 us (25%)
  starting transfers between devices  26 us (10%)
  matrix products  23.9 us (10%)
  between operations  17.1 us (7%)
  other arithmetic  16.3 us (7%)
  blocking collectives  14.3 us (6%)
  loops' own time  7.15 us (3%)
    all_gather x1, waiting for transfers between devices, body(): shards = lax.all_gather(ref_feats, 'qry', axis=1, tiled=True)  62.7 us
    dot_general x1, matrix products, frame_sims(): lax.dot_general(query_mat, ref_mat, (((1,), (1,)), ((), ())), preferred_e...  18.8 us
    ppermute x6, starting transfers between devices, padded_2(): lax.ppermute(lax.slice_in_dim(block, block.shape[dim] - width, None, axis...  18 us
    ppermute x6, waiting for transfers between devices, padded_2(): lax.ppermute(lax.slice_in_dim(block, 0, width, axis=dim), axis, backward)  16.2 us
    dot_general x1, local copies, waits for them, and re-layouts, frame_sims(): lax.dot_general(query_mat, ref_mat, (((1,), (1,)), ((), ())), preferred_e...  12.7 us
    reduce_max x8, other arithmetic, one_block(): jnp.max(result.reshape(outputs, block_rows // 2, 2, width // 2, 2), axis=...  12.3 us
    while x76, local copies, waits for them, and re-layouts  11.5 us
    concatenate x10, local copies, waits for them, and re-layouts, one_block(): jnp.concatenate([window[:, shift_row:shift_row + block_rows, shift_col:sh...  11 us
  transfers between devices with their start and end apart: 13, of which 8 were waited for; matrix products, arithmetic and copies ran while one was open for 2% of the time, Pallas kernels for 0%

commit v1 on v0

v1 whole, which is shorter than its diff:
```python
import functools
import math

import jax
import jax.numpy as jnp
import numpy as np
from jax import lax
from jax.experimental import pallas as pl
from jax.experimental.pallas import tpu as pltpu
from jax.sharding import PartitionSpec as P

PIECE = 8
PHASES = 4
HALO = 2
JP = 48
GROUP = 3
WINDOW = PHASES * GROUP + 2
BF = jnp.bfloat16
F32 = jnp.float32


def shift(array, axis, pairs):
    return lax.ppermute(array, axis, pairs)


def sims_kernel(scale, regions, counts, pos_ref, table_ref, query_ref, *refs):
    pieces, outs = refs[: len(counts)], refs[len(counts) :]
    step = pl.program_id(0)
    width = query_ref.shape[0]
    active = table_ref[pos_ref[0], pos_ref[1]] == 1
    factor = jnp.where(active, scale, 0.0).astype(F32)
    for count, piece, out in zip(counts, pieces, outs):
        products = lax.dot_general(
            piece[...],
            query_ref[...].reshape(-1, query_ref.shape[2]),
            (((1,), (1,)), ((), ())),
            preferred_element_type=F32,
        )
        best = products[0:count]
        for other in range(1, regions):
            best = jnp.maximum(best, products[other * count : (other + 1) * count])
        frames = query_ref.shape[1]
        total = best[:, 0:frames]
        for other in range(1, width):
            total = total + best[:, other * frames : (other + 1) * frames]
        total = total * factor

        @pl.when(step == 0)
        def _():
            out[...] = total

        @pl.when(step > 0)
        def _():
            out[...] += total


def similarities(query, pieces, position, table):
    regions, frames, channels = query.shape
    counts = [piece.shape[0] // regions for piece in pieces]
    width = 3 if regions % 3 == 0 else 1
    scale = 1.0 / (regions * math.sqrt(channels))
    rows = sum(piece.shape[0] for piece in pieces)
    return pl.pallas_call(
        functools.partial(sims_kernel, scale, regions, counts),
        grid=(regions // width,),
        in_specs=[
            pl.BlockSpec(memory_space=pltpu.SMEM),
            pl.BlockSpec(memory_space=pltpu.SMEM),
            pl.BlockSpec((width, frames, channels), lambda i: (i, 0, 0)),
        ]
        + [pl.BlockSpec(piece.shape, lambda i: (0, 0)) for piece in pieces],
        out_specs=[pl.BlockSpec((count, frames), lambda i: (0, 0)) for count in counts],
        out_shape=[jax.ShapeDtypeStruct((count, frames), F32) for count in counts],
        cost_estimate=pl.CostEstimate(
            flops=2 * rows * regions * frames * channels,
            bytes_accessed=2 * channels * (rows + regions * frames),
            transcendentals=0,
        ),
        name="similarities",
    )(position, table, query, *pieces)


def network_kernel(
    map_rows,
    map_cols,
    pos_ref,
    len_ref,
    own_ref,
    left_ref,
    right_ref,
    top_ref,
    bottom_ref,
    w1_ref,
    b1_ref,
    w2_ref,
    b2_ref,
    w3_ref,
    b3_ref,
    w4_ref,
    b4_ref,
    score_ref,
    peak_ref,
    sims_ref,
    y_ref,
    first_ref,
    lhs2_ref,
    second_ref,
    lhs3_ref,
    flat_ref,
):
    block = own_ref.shape[1]
    frames = own_ref.shape[2]
    cells = block + 2 * HALO
    groups = cells // GROUP
    row0 = pos_ref[0] * block
    col0 = pos_ref[1] * block
    videos = len_ref.shape[0]

    lanes = sims_ref.shape[2]
    edge = top_ref.shape[2]
    sims_ref[...] = jnp.zeros_like(sims_ref)
    sims_ref[:, 3 : 3 + block, 0:frames] = own_ref[...]
    sims_ref[:, 1:3, 0:frames] = left_ref[...]
    sims_ref[:, 3 + block : 5 + block, 0:frames] = right_ref[...]
    sims_ref[:, 1 : 1 + cells, frames : frames + edge] = bottom_ref[...]
    sims_ref[:, 1 : 1 + cells, lanes - edge : lanes] = top_ref[...]

    sources = [(PHASES - 1, 0)] + [(phase, 1) for phase in range(PHASES)] + [(0, 2)]
    bases = [sims_ref[phase, at : at + JP, :] for phase, at in sources]
    zero = jnp.zeros((JP, 128 - len(sources) * WINDOW), F32)
    reach = PHASES * HALO + 1
    for group in range(groups):
        low = PHASES * GROUP * group - reach
        parts = []
        for base in bases:
            if low < 0:
                parts.append(base[:, lanes + low : lanes])
                parts.append(base[:, 0 : low + WINDOW])
            else:
                parts.append(base[:, low : low + WINDOW])
        window = jnp.concatenate(parts + [zero], axis=1)
        high = window.astype(BF)
        rest = (window - high.astype(F32)).astype(BF)
        y_ref[group * JP : (group + 1) * JP, 0:128] = high
        y_ref[group * JP : (group + 1) * JP, 128:256] = rest
        y_ref[group * JP : (group + 1) * JP, 256:384] = high

    cell = lax.broadcasted_iota(jnp.int32, (JP, 128), 0)
    lane = lax.broadcasted_iota(jnp.int32, (JP, 128), 1)

    def inside(halo):
        at = cell + (col0 - halo)
        return jnp.where((at >= 0) & (at < map_cols), 1.0, 0.0).astype(F32)

    def row_flag(at):
        return jnp.where((at >= 0) & (at < map_rows), 1.0, 0.0).astype(F32)

    cols_first = inside(HALO)
    for member in range(GROUP):
        result = jnp.dot(
            y_ref[...], w1_ref[:, member * 512 : (member + 1) * 512], preferred_element_type=F32
        )
        pooled = jnp.maximum(
            jnp.maximum(result[:, 0:128], result[:, 128:256]),
            jnp.maximum(result[:, 256:384], result[:, 384:512]),
        )
        pooled = jnp.maximum(pooled + b1_ref[...], 0.0)
        for group in range(groups):
            at = group * GROUP + member
            keep = cols_first * row_flag(row0 + at - HALO)
            first_ref[at] = (pooled[group * JP : (group + 1) * JP] * keep).astype(BF).astype(F32)

    upper = lane < 64
    left = (lane // 32) % 2 == 0
    rows2 = block + 2
    for at in range(rows2):
        centre = first_ref[at + 1]
        across = jnp.where(upper, first_ref[at + 2], first_ref[at])
        for index, value in enumerate((centre, across)):
            here = pltpu.roll(value, JP - 1, 0)
            beside = jnp.where(left, pltpu.roll(value, JP - 2, 0), value)
            lhs2_ref[at * JP : (at + 1) * JP, index * 256 : index * 256 + 128] = here.astype(BF)
            lhs2_ref[at * JP : (at + 1) * JP, index * 256 + 128 : index * 256 + 256] = (
                beside.astype(BF)
            )
    result = jnp.dot(lhs2_ref[...], w2_ref[...], preferred_element_type=F32)
    pooled = jnp.maximum(result[:, 0:128], result[:, 128:256])
    pooled = jnp.maximum(pooled, pltpu.roll(pooled, 64, 1))
    pooled = jnp.maximum(pooled + b2_ref[...], 0.0)
    cols_second = inside(1)
    for at in range(rows2):
        keep = cols_second * row_flag(row0 + at - 1)
        second_ref[at] = (pooled[at * JP : (at + 1) * JP] * keep).astype(BF).astype(F32)

    upper = lane[0:block] < 64
    for at in range(block):
        row = slice(at * block, (at + 1) * block)
        for down in range(3):
            value = second_ref[at + down]
            pair = jnp.where(upper, value[0:block], value[1 : 1 + block])
            lhs3_ref[row, down * 128 : (down + 1) * 128] = pair.astype(BF)
        pair = jnp.where(
            upper, second_ref[at, 2 : 2 + block, :], second_ref[at + 1, 2 : 2 + block, :]
        )
        lhs3_ref[row, 384:512] = pair.astype(BF)
        lhs3_ref[row, 512:640] = second_ref[at + 2, 2 : 2 + block, :].astype(BF)
    third = jnp.dot(lhs3_ref[...], w3_ref[...], preferred_element_type=F32)
    third = jnp.maximum(third + b3_ref[...], 0.0).astype(BF)
    flat = lax.dot_general(
        w4_ref[...], third, (((1,), (1,)), ((), ())), preferred_element_type=F32
    )
    flat_ref[...] = flat[0:8] + b4_ref[0]
    for at in range(block):
        score_ref[at : at + 1, :] = flat_ref[0:1, at * block : (at + 1) * block]

    score = score_ref[...]
    column = col0 + lax.broadcasted_iota(jnp.int32, (block, block), 1)
    slot = lax.broadcasted_iota(jnp.int32, (block, videos), 1)
    start = jnp.int32(0)
    peaks = jnp.zeros((block, videos), F32)
    for video in range(videos):
        end = start + len_ref[video]
        member = (column >= start) & (column < end)
        best = jnp.max(jnp.where(member, score, -jnp.inf), axis=1, keepdims=True)
        peaks = jnp.where(slot == video, best, peaks)
        start = end
    peak_ref[...] = peaks


def network(position, lengths, own, left, right, top, bottom, weights, map_rows, map_cols):
    block = own.shape[1]
    frames = own.shape[2]
    cells = block + 2 * HALO
    videos = lengths.shape[0]
    smem = pl.BlockSpec(memory_space=pltpu.SMEM)
    vmem = pl.BlockSpec(memory_space=pltpu.VMEM)
    w1, b1, w2, b2, w3, b3, w4, b4 = weights
    return pl.pallas_call(
        functools.partial(network_kernel, map_rows, map_cols),
        in_specs=[smem, smem] + [vmem] * 5 + [vmem] * 7 + [smem],
        out_specs=[vmem, vmem],
        out_shape=[
            jax.ShapeDtypeStruct((block, block), F32),
            jax.ShapeDtypeStruct((block, videos), F32),
        ],
        scratch_shapes=[
            pltpu.VMEM((PHASES, JP + 8, 2 * frames), F32),
            pltpu.VMEM((cells // GROUP * JP, 384), BF),
            pltpu.VMEM((cells, JP, 128), F32),
            pltpu.VMEM(((block + 2) * JP, 512), BF),
            pltpu.VMEM((block + 2, JP, 128), F32),
            pltpu.VMEM((block * block, 640), BF),
            pltpu.VMEM((8, block * block), F32),
        ],
        cost_estimate=pl.CostEstimate(
            flops=2_000_000_000, bytes_accessed=4_000_000, transcendentals=0
        ),
        name="network",
    )(position, lengths, own, left, right, top, bottom, w1, b1, w2, b2, w3, b3, w4, b4)


def network_weights(w1, b1, w2, b2, w3, b3, w4, b4):
    c1, c2, c3 = w1.shape[2], w2.shape[2], w3.shape[2]
    rows = np.arange(6 * WINDOW)
    member, pr, pc, sr, sc, _ = np.unravel_index(
        np.arange(GROUP * 16 * c1), (GROUP, 2, 2, 2, 2, c1)
    )
    down = jnp.asarray(rows % WINDOW, jnp.int32)[:, None] - jnp.asarray(
        PHASES * member + 2 * sr + pr, jnp.int32
    )
    along = jnp.asarray(rows // WINDOW, jnp.int32)[:, None] - jnp.asarray(2 * sc + pc, jnp.int32)
    tiled = jnp.tile(w1.astype(F32), (1, 1, GROUP * 16))
    dense = jnp.zeros((6 * WINDOW, GROUP * 16 * c1), F32)
    for di in range(3):
        for dj in range(3):
            dense = jnp.where((down == di) & (along == dj), tiled[di, dj][None, :], dense)
    dense = jnp.pad(dense, ((0, 128 - 6 * WINDOW), (0, 0)))
    high = lax.reduce_precision(dense, 8, 7)
    rest = (dense - high).astype(BF)
    high = high.astype(BF)
    first = jnp.concatenate([high, high, rest], axis=0)
    taps = jnp.transpose(w2, (0, 1, 3, 2))
    nothing = jnp.zeros((c1, c2), w2.dtype)
    reach = ((0, 1), (2, -1))
    columns = []
    for qr in range(2):
        for qc in range(2):
            column = []
            for row_kind in range(2):
                for col_kind in range(2):
                    for sr in range(2):
                        for sc in range(2):
                            di = reach[row_kind][sr] - qr + 1
                            dj = reach[col_kind][sc] - qc + 1
                            fits = 0 <= di <= 2 and 0 <= dj <= 2
                            column.append(taps[di, dj] if fits else nothing)
            columns.append(jnp.concatenate(column, axis=0))
    second = jnp.concatenate(columns, axis=1)
    taps = jnp.transpose(w3, (0, 1, 3, 2))
    order = [(0, 0), (0, 1), (1, 0), (1, 1), (2, 0), (2, 1), (0, 2), (1, 2), (2, 2)]
    third = jnp.concatenate(
        [taps[di, dj] for di, dj in order] + [jnp.zeros((c2, c3), w3.dtype)], axis=0
    )
    fourth = jnp.broadcast_to(w4[None], (16, c3))
    return (
        first,
        jnp.tile(b1, 128 // c1)[None],
        second,
        jnp.tile(b2, 128 // c2)[None],
        third,
        b3[None],
        fourth,
        b4,
    )


def body(
    query_feats,
    ref_feats,
    pair_table,
    lengths,
    query_len,
    conv1_weight,
    conv1_bias,
    conv2_weight,
    conv2_bias,
    conv3_weight,
    conv3_bias,
    conv4_weight,
    conv4_bias,
):
    qry_index = lax.axis_index("qry")
    ref_index = lax.axis_index("ref")
    senders = lax.axis_size("qry")
    blocks = lax.axis_size("ref")
    position = jnp.stack([qry_index, ref_index]).astype(jnp.int32)
    frames, regions, channels = query_feats.shape
    rows = ref_feats.shape[0]
    query = jnp.transpose(query_feats, (1, 0, 2))
    own = jnp.transpose(ref_feats[:, 0], (1, 0, 2))
    chips = senders // 2
    count = rows // PIECE
    order = [0, count - 1] + list(range(1, count - 1)) if count > 1 else [0]
    pieces = [
        own[:, at * PIECE : (at + 1) * PIECE].reshape(regions * PIECE, channels) for at in order
    ]
    across = [
        [(i, (i - 2 * step) % senders) for i in range(senders)] for step in range(1, chips)
    ]
    beside = [(i, i ^ 1) for i in range(senders)]

    whole = own.reshape(regions * rows, channels)
    found = [[shift(piece, "qry", pairs) for piece in pieces] for pairs in across]
    sibling = shift(whole, "qry", beside)
    tile = [similarities(query, [whole], position, pair_table)[0]]
    tile.append(similarities(query, [sibling], position, pair_table)[0])
    for group in found:
        here, there = [None] * count, [None] * count
        for at, piece in zip(order, group):
            other = shift(piece, "qry", beside)
            here[at], there[at] = similarities(query, [piece, other], position, pair_table)
        tile.append(jnp.concatenate(here, axis=0))
        tile.append(jnp.concatenate(there, axis=0))
    relative = jnp.stack(tile)
    sender = jnp.arange(senders, dtype=jnp.int32)
    step = (sender // 2 - qry_index // 2) % chips
    source = 2 * step + (sender % 2) ^ (qry_index % 2)
    ordered = relative[source]
    sims = (
        ordered.reshape(senders // PHASES, PHASES, rows, frames)
        .transpose(1, 2, 0, 3)
        .reshape(PHASES, frames // PHASES, frames)
    )
    up = [(i, i + 1) for i in range(blocks - 1)]
    down = [(b, a) for a, b in up]
    left = shift(sims[:, -HALO:], "ref", up)
    right = shift(sims[:, :HALO], "ref", down)
    wide = jnp.concatenate([left, sims, right], axis=1)
    up = [(i, i + 1) for i in range(senders - 1)]
    down = [(b, a) for a, b in up]
    top = shift(wide[:, :, frames - 8 :], "qry", up)
    bottom = shift(wide[:, :, :8], "qry", down)
    weights = network_weights(
        conv1_weight,
        conv1_bias,
        conv2_weight,
        conv2_bias,
        conv3_weight,
        conv3_bias,
        conv4_weight,
        conv4_bias,
    )
    block = frames // PHASES
    score_map, peaks = network(
        position, lengths, sims, left, right, top, bottom, weights, block * senders, block * blocks
    )
    best = peaks
    for step in range(1, blocks):
        pairs = [(i, (i + step) % blocks) for i in range(blocks)]
        best = jnp.maximum(best, shift(peaks, "ref", pairs))
    row_ids = qry_index * block + jnp.arange(block, dtype=jnp.int32)
    partial = jnp.sum(jnp.where((row_ids < query_len[0])[:, None], best, 0.0), axis=0)
    total = partial
    for step in range(1, senders):
        pairs = [(i, (i + step) % senders) for i in range(senders)]
        total = total + shift(partial, "qry", pairs)
    return (score_map, total / query_len[0].astype(F32))


def solution(mesh):
    placed = (
        P(("groups", "qry"), None, None),
        P(("groups", "ref"), "qry", None, None),
        P("groups", None),
        P("groups"),
        P("groups"),
    ) + (P(),) * 8
    return jax.shard_map(
        body,
        mesh=mesh,
        in_specs=placed,
        out_specs=(P(("groups", "qry"), "ref"), P("groups")),
        check_vma=False,
    )
```

time: 250 us -> 149 us (0.60)
  Pallas kernels: 0 us -> 61.5 us
  waiting for transfers between devices: 80 us -> 26.3 us
  local copies, waits for them, and re-layouts: 63.7 us -> 28.1 us
  matrix products: 23.9 us -> 0 us
  between operations: 17.1 us -> 2.38 us
  blocking collectives: 14.3 us -> 0 us
  other arithmetic: 16.3 us -> 7.09 us
  loops' own time: 7.15 us -> 0 us
  starting transfers between devices: 26 us -> 22.5 us
    all_gather x1 -> x0, waiting for transfers between devices: 62.7 us -> none  [body(): shards = lax.all_gather(ref_feats, 'qry', axis=1, tiled=True)]
    pallas_call x0 -> x7, Pallas kernels: none -> 61.5 us  [the longest x6 55.9 us: similarities(): pl.pallas_call(functools.partial(sims_kernel, scale, regions, counts), gr...]
    dot_general x12 -> x0, matrix products: 23.9 us -> none  [the longest x1 18.8 us: frame_sims(): lax.dot_general(query_mat, ref_mat, (((1,), (1,)), ((), ())), preferred_e...]
    unnamed x16 -> x98, local copies, waits for them, and re-layouts: 0.04 us -> 20.4 us
    dot_general x1 -> x0, local copies, waits for them, and re-layouts: 12.7 us -> none  [frame_sims(): lax.dot_general(query_mat, ref_mat, (((1,), (1,)), ((), ())), preferred_e...]
    while x78 -> x0, local copies, waits for them, and re-layouts: 12.7 us -> none
    reduce_max x9 -> x0, other arithmetic: 12.4 us -> none  [the longest x8 12.3 us: one_block(): jnp.max(result.reshape(outputs, block_rows // 2, 2, width // 2, 2), axis=...]
    ppermute x12 -> x19, waiting for transfers between devices: 16.6 us -> 26.3 us  [shift(): return lax.ppermute(array, axis, pairs)]
  transfers between devices with their start and end apart: 13 -> 19, of which waited for: 8 -> 8; matrix products, arithmetic and copies ran while one was open for 2% -> 18% of each run, Pallas kernels for 0% -> 33%
where the time goes in v1:
time: 149 us; the launch traced here: 148 us
  Pallas kernels  61.5 us (41%)
  local copies, waits for them, and re-layouts  28.1 us (19%)
  waiting for transfers between devices  26.3 us (18%)
  starting transfers between devices  22.5 us (15%)
  other arithmetic  7.09 us (5%)
  between operations  2.38 us (2%)
    pallas_call x6, Pallas kernels, similarities(): pl.pallas_call(functools.partial(sims_kernel, scale, regions, counts), gr...  55.9 us
    ppermute x19, waiting for transfers between devices, shift(): return lax.ppermute(array, axis, pairs)  26.3 us
    ppermute x19, starting transfers between devices, shift(): return lax.ppermute(array, axis, pairs)  22.5 us
    unnamed x98, local copies, waits for them, and re-layouts  20.4 us
    pallas_call x1, Pallas kernels, network(): pl.pallas_call(functools.partial(network_kernel, map_rows, map_cols), in_...  5.63 us
    reshape x1, local copies, waits for them, and re-layouts, body(): own[:, at * PIECE:(at + 1) * PIECE].reshape(regions * PIECE, channels)  3.08 us
  transfers between devices with their start and end apart: 19, of which 8 were waited for; matrix products, arithmetic and copies ran while one was open for 18% of the time, Pallas kernels for 33%

profile of v1, /device:TPU:0, one launch (start us, length us, event | category | flops | bytes accessed | tf_op | source)
XLA Modules:
  0.0 147.8 jit_solution(7778383539019226785)
XLA Ops:
  0.7 3.1 %slice_bitcast_fusion.3 = (bf16[72,3840]{1,0:T(8,128)(2,1)}, bf16[72,3840]{1,0:T(8,128)(2,1)}, bf16[72,3840]{1,0:T(8,128)(2,1)}, bf16[72,3840]{1,0:T(8,128)(2,1)}) fusion(bf16[9,32,3840]{2,1,0:T(8,128)(2,1)} %bitcast.164), kind=kLoop, calls=%fused_computation.23 | loop fusion | bytes 4423680 | tf_op jit(solution)/shard_map/reshape | solution.py:345
  3.8 3.0 %collective-permute-start.7 = (bf16[72,3840]{1,0:T(8,128)(2,1)}, bf16[72,3840]{1,0:T(8,128)(2,1)}, u32[]{:S(2)}, u32[]{:S(2)}) collective-permute-start(bf16[72,3840]{1,0:T(8,128)(2,1)} %get-tuple-element.34), channel_id=1, source_target_pairs={{0,8},{4,12},{8,0},{12,4},{1,9},{5,13},{9,1},{13,5},{2,10},{6,14},... | collective-permute-start | bytes 1658888 | tf_op jit(solution)/shard_map/ppermute | solution.py:23
  6.8 2.0 %collective-permute-start.3 = (bf16[72,3840]{1,0:T(8,128)(2,1)}, bf16[72,3840]{1,0:T(8,128)(2,1)}, u32[]{:S(2)}, u32[]{:S(2)}) collective-permute-start(bf16[72,3840]{1,0:T(8,128)(2,1)} %get-tuple-element.33), channel_id=1, source_target_pairs={{0,8},{4,12},{8,0},{12,4},{1,9},{5,13},{9,1},{13,5},{2,10},{6,14},... | collective-permute-start | bytes 1658888 | tf_op jit(solution)/shard_map/ppermute | solution.py:23
  27.3 7.6 %similarities.6 = f32[32,128]{1,0:T(8,128)} custom-call(s32[2]{0:T(128)} %pad_add_fusion.pos_ref, s32[4,4]{1,0:T(4,128)} %table_ref.11, bf16[9,128,3840]{2,1,0:T(8,128)(2,1)} %bitcast.158, bf16[288,3840]{1,0:T(8,128)(2,1)} %bitcast.165), custom_call_target="tpu_custom_call" | custom-call | flops 2548039680 | bytes 11059200 | tf_op jit(solution)/shard_map/similarities/pallas_call | solution.py:63
  36.1 1.3 constant_dynamic-update-slice_fusion.54
  38.6 5.6 %collective-permute-done.3.refs_0_ = bf16[72,3840]{1,0:T(8,128)(2,1)} collective-permute-done((bf16[72,3840]{1,0:T(8,128)(2,1)}, bf16[72,3840]{1,0:T(8,128)(2,1)}, u32[]{:S(2)}, u32[]{:S(2)}) %collective-permute-start.3) | collective-permute-done | bytes 552992 | tf_op jit(solution)/shard_map/ppermute | solution.py:23
  44.2 11.0 %collective-permute-done.1.refs_0_ = bf16[72,3840]{1,0:T(8,128)(2,1)} collective-permute-done((bf16[72,3840]{1,0:T(8,128)(2,1)}, bf16[72,3840]{1,0:T(8,128)(2,1)}, u32[]{:S(2)}, u32[]{:S(2)}) %collective-permute-start.1) | collective-permute-done | bytes 552992 | tf_op jit(solution)/shard_map/ppermute | solution.py:23
  57.3 10.1 %similarities.11 = (f32[8,128]{1,0:T(8,128)}, f32[8,128]{1,0:T(8,128)}) custom-call(s32[2]{0:T(128)} %pad_add_fusion.pos_ref, s32[4,4]{1,0:T(4,128)} %table_ref.11, bf16[9,128,3840]{2,1,0:T(8,128)(2,1)} %bitcast.159, bf16[72,3840]{1,0:T(8,128)(2,1)} %collective-permute-done.7.refs_0_, bf16[72,3840]{1,0:T(8,128)(2,1)} %copy-done.2), custom_call_target="tpu_custom_call" | custom-call | flops 1274019840 | bytes 9953280 | tf_op jit(solution)/shard_map/similarities/pallas_call | solution.py:63
  68.2 10.1 %similarities.10 = (f32[8,128]{1,0:T(8,128)}, f32[8,128]{1,0:T(8,128)}) custom-call(s32[2]{0:T(128)} %pad_add_fusion.pos_ref, s32[4,4]{1,0:T(4,128)} %table_ref.11, bf16[9,128,3840]{2,1,0:T(8,128)(2,1)} %bitcast.160, bf16[72,3840]{1,0:T(8,128)(2,1)} %collective-permute-done.5.refs_0_, bf16[72,3840]{1,0:T(8,128)(2,1)} %copy-done.3), custom_call_target="tpu_custom_call" | custom-call | flops 1274019840 | bytes 9953280 | tf_op jit(solution)/shard_map/similarities/pallas_call | solution.py:63
  78.3 10.1 %similarities.9 = (f32[8,128]{1,0:T(8,128)}, f32[8,128]{1,0:T(8,128)}) custom-call(s32[2]{0:T(128)} %pad_add_fusion.pos_ref, s32[4,4]{1,0:T(4,128)} %table_ref.11, bf16[9,128,3840]{2,1,0:T(8,128)(2,1)} %bitcast.161, bf16[72,3840]{1,0:T(8,128)(2,1)} %collective-permute-done.3.refs_0_, bf16[72,3840]{1,0:T(8,128)(2,1)} %collective-permute-done.4.refs_1_), custom_call_target="tpu_custom_call" | custom-call | flops 1274019840 | bytes 9953280 | tf_op jit(solution)/shard_map/similarities/pallas_call | solution.py:63
  88.5 10.1 %similarities.8 = (f32[8,128]{1,0:T(8,128)}, f32[8,128]{1,0:T(8,128)}) custom-call(s32[2]{0:T(128)} %pad_add_fusion.pos_ref, s32[4,4]{1,0:T(4,128)} %table_ref.11, bf16[9,128,3840]{2,1,0:T(8,128)(2,1)} %bitcast.162, bf16[72,3840]{1,0:T(8,128)(2,1)} %collective-permute-done.1.refs_0_, bf16[72,3840]{1,0:T(8,128)(2,1)} %collective-permute-done.2.refs_1_), custom_call_target="tpu_custom_call" | custom-call | flops 1274019840 | bytes 9953280 | tf_op jit(solution)/shard_map/similarities/pallas_call | solution.py:63
  99.4 7.7 %similarities.7 = f32[32,128]{1,0:T(8,128)} custom-call(s32[2]{0:T(128)} %pad_add_fusion.pos_ref, s32[4,4]{1,0:T(4,128)} %table_ref.11, bf16[9,128,3840]{2,1,0:T(8,128)(2,1)} %bitcast.163, bf16[288,3840]{1,0:T(8,128)(2,1)} %collective-permute-done.refs_0_), custom_call_target="tpu_custom_call" | custom-call | flops 2548039680 | bytes 11059200 | tf_op jit(solution)/shard_map/similarities/pallas_call | solution.py:63
  108.5 3.7 %collective-permute-start.9 = (f32[4,2,128]{2,1,0:T(2,128)S(1)}, f32[4,2,128]{2,1,0:T(2,128)S(1)}, u32[]{:S(2)}, u32[]{:S(2)}) collective-permute-start(f32[4,2,128]{2,1,0:T(2,128)S(1)} %get-tuple-element.62), channel_id=1, source_target_pairs={{0,1},{1,2},{2,3},{4,5},{5,6},{6,7},{8,9},{9,10},{10,11},{12,13},{... | collective-permute-start | bytes 12296 | tf_op jit(solution)/shard_map/ppermute | solution.py:23
  113.5 1.8 %pad_maximum_fusion.1.w2_ref = bf16[512,256]{1,0:T(8,128)(2,1)} fusion(bf16[512,64]{1,0:T(8,128)(2,1)S(1)} %constant_dynamic-update-slice_fusion.39, bf16[512,64]{1,0:T(8,128)(2,1)S(1)} %copy-done.6, bf16[512,64]{1,0:T(8,128)(2,1)} %constant_dynamic-update-slice_fusion.13, bf16[512,64]{1,0:T(8,128)(2,1)S(1)} %copy-done.8), kind=kLoop, calls=%fused_computation.25 | loop fusion | flops 1048576 | bytes 524288 | tf_op jit(solution)/shard_map/concatenate | solution.py:298
  115.3 2.4 %collective-permute-done.10.right_ref = f32[4,2,128]{2,1,0:T(2,128)S(1)} collective-permute-done((f32[4,2,128]{2,1,0:T(2,128)S(1)}, f32[4,2,128]{2,1,0:T(2,128)S(1)}, u32[]{:S(2)}, u32[]{:S(2)}) %collective-permute-start.10) | collective-permute-done | bytes 4128 | tf_op jit(solution)/shard_map/ppermute | solution.py:23
  119.1 1.5 collective-permute-start.12
  124.7 5.6 %network.1 = (f32[32,32]{1,0:T(8,128)}, f32[32,2]{1,0:T(8,128)}) custom-call(s32[2]{0:T(128)} %pad_add_fusion.pos_ref, s32[2]{0:T(128)} %len_ref.1, f32[4,32,128]{2,1,0:T(8,128)} %copy-done.4, f32[4,2,128]{2,1,0:T(2,128)} %copy-done.13, f32[4,2,128]{2,1,0:T(2,128)} %copy-done.14, f32[4,36,8]{2,1,0:T(8,128)} %copy-done.25, f32[4,36,8]{2,1,0:T(8,128)} %copy-done.26, ...), custom_call_target="tpu_custom_call" | custom-call | flops 2000000000 | bytes 4000000 | tf_op jit(solution)/shard_map/network/pallas_call | solution.py:238
  130.3 2.6 %collective-permute-start.15 = (f32[32,2]{1,0:T(8,128)}, f32[32,2]{1,0:T(8,128)S(1)}, u32[]{:S(2)}, u32[]{:S(2)}) collective-permute-start(f32[32,2]{1,0:T(8,128)} %get-tuple-element.21), channel_id=1, source_target_pairs={{0,3},{1,0},{2,1},{3,2},{4,7},{5,4},{6,5},{7,6},{8,11},{9,8},{10,9... | collective-permute-start | bytes 776 | tf_op jit(solution)/shard_map/ppermute | solution.py:23
  133.4 1.6 %collective-permute-start.13 = (f32[32,2]{1,0:T(8,128)}, f32[32,2]{1,0:T(8,128)S(1)}, u32[]{:S(2)}, u32[]{:S(2)}) collective-permute-start(f32[32,2]{1,0:T(8,128)} %get-tuple-element.21), channel_id=1, source_target_pairs={{0,1},{1,2},{2,3},{3,0},{4,5},{5,6},{6,7},{7,4},{8,9},{9,10},{10,1... | collective-permute-start | bytes 776 | tf_op jit(solution)/shard_map/ppermute | solution.py:23
  135.0 2.8 %collective-permute-done.14 = f32[32,2]{1,0:T(8,128)S(1)} collective-permute-done((f32[32,2]{1,0:T(8,128)}, f32[32,2]{1,0:T(8,128)S(1)}, u32[]{:S(2)}, u32[]{:S(2)}) %collective-permute-start.14) | collective-permute-done | bytes 288 | tf_op jit(solution)/shard_map/ppermute | solution.py:23
  137.8 1.3 collective-permute-done.13
  141.0 3.3 %collective-permute-start.17 = (f32[2]{0:T(128)S(1)}, f32[2]{0:T(128)S(1)}, u32[]{:S(2)}, u32[]{:S(2)}) collective-permute-start(f32[2]{0:T(128)S(1)} %select_reduce_fusion), channel_id=1, source_target_pairs={{0,8},{4,12},{8,0},{12,4},{1,9},{5,13},{9,1},{13,5},{2,10},{6,14},... | collective-permute-start | bytes 32 | tf_op jit(solution)/shard_map/ppermute | solution.py:23
  144.4 1.4 collective-permute-done.17
  145.8 1.4 collective-permute-done.16
  (149 shorter events, 34.2 us)
Async XLA Ops:
  3.8 33.7 %collective-permute-start.7 = (bf16[72,3840]{1,0:T(8,128)(2,1)}, bf16[72,3840]{1,0:T(8,128)(2,1)}, u32[]{:S(2)}, u32[]{:S(2)}) collective-permute-start(bf16[72,3840]{1,0:T(8,128)(2,1)} %get-tuple-element.34), channel_id=1, source_target_pairs={{0,8},{4,12},{8,0},{12,4},{1,9},{5,13},{9,1},{13,5},{2,10},{6,14},... | collective-permute-start | bytes 1658888 | tf_op jit(solution)/shard_map/ppermute | solution.py:23
  6.8 31.8 %collective-permute-start.5 = (bf16[72,3840]{1,0:T(8,128)(2,1)}, bf16[72,3840]{1,0:T(8,128)(2,1)}, u32[]{:S(2)}, u32[]{:S(2)}) collective-permute-start(bf16[72,3840]{1,0:T(8,128)(2,1)} %get-tuple-element.32), channel_id=1, source_target_pairs={{0,8},{4,12},{8,0},{12,4},{1,9},{5,13},{9,1},{13,5},{2,10},{6,14},... | collective-permute-start | bytes 1658888 | tf_op jit(solution)/shard_map/ppermute | solution.py:23
  6.8 37.3 %collective-permute-start.3 = (bf16[72,3840]{1,0:T(8,128)(2,1)}, bf16[72,3840]{1,0:T(8,128)(2,1)}, u32[]{:S(2)}, u32[]{:S(2)}) collective-permute-start(bf16[72,3840]{1,0:T(8,128)(2,1)} %get-tuple-element.33), channel_id=1, source_target_pairs={{0,8},{4,12},{8,0},{12,4},{1,9},{5,13},{9,1},{13,5},{2,10},{6,14},... | collective-permute-start | bytes 1658888 | tf_op jit(solution)/shard_map/ppermute | solution.py:23
  8.8 46.4 %collective-permute-start.1 = (bf16[72,3840]{1,0:T(8,128)(2,1)}, bf16[72,3840]{1,0:T(8,128)(2,1)}, u32[]{:S(2)}, u32[]{:S(2)}) collective-permute-start(bf16[72,3840]{1,0:T(8,128)(2,1)} %get-tuple-element.31), channel_id=1, source_target_pairs={{0,8},{4,12},{8,0},{12,4},{1,9},{5,13},{9,1},{13,5},{2,10},{6,14},... | collective-permute-start | bytes 1658888 | tf_op jit(solution)/shard_map/ppermute | solution.py:23
  8.8 90.6 %collective-permute-start = (bf16[288,3840]{1,0:T(8,128)(2,1)S(1)}, bf16[288,3840]{1,0:T(8,128)(2,1)}, u32[]{:S(2)}, u32[]{:S(2)}) collective-permute-start(bf16[288,3840]{1,0:T(8,128)(2,1)S(1)} %bitcast.166), channel_id=1, source_target_pairs={{0,4},{4,0},{8,12},{12,8},{1,5},{5,1},{9,13},{13,9},{2,6},{6,2},{1... | collective-permute-start | bytes 6635528 | tf_op jit(solution)/shard_map/ppermute | solution.py:23
  37.5 19.0 %collective-permute-start.8 = (bf16[72,3840]{1,0:T(8,128)(2,1)}, bf16[72,3840]{1,0:T(8,128)(2,1)S(1)}, u32[]{:S(2)}, u32[]{:S(2)}) collective-permute-start(bf16[72,3840]{1,0:T(8,128)(2,1)} %collective-permute-done.7.refs_0_), channel_id=1, source_target_pairs={{0,4},{4,0},{8,12},{12,8},{1,5},{5,1},{9,13},{13,9},{2,6},{6,2},{1... | collective-permute-start | bytes 1658888 | tf_op jit(solution)/shard_map/ppermute | solution.py:23
  38.5 28.8 %collective-permute-start.6 = (bf16[72,3840]{1,0:T(8,128)(2,1)}, bf16[72,3840]{1,0:T(8,128)(2,1)S(1)}, u32[]{:S(2)}, u32[]{:S(2)}) collective-permute-start(bf16[72,3840]{1,0:T(8,128)(2,1)} %collective-permute-done.5.refs_0_), channel_id=1, source_target_pairs={{0,4},{4,0},{8,12},{12,8},{1,5},{5,1},{9,13},{13,9},{2,6},{6,2},{1... | collective-permute-start | bytes 1658888 | tf_op jit(solution)/shard_map/ppermute | solution.py:23
  44.2 34.2 %collective-permute-start.4 = (bf16[72,3840]{1,0:T(8,128)(2,1)}, bf16[72,3840]{1,0:T(8,128)(2,1)}, u32[]{:S(2)}, u32[]{:S(2)}) collective-permute-start(bf16[72,3840]{1,0:T(8,128)(2,1)} %collective-permute-done.3.refs_0_), channel_id=1, source_target_pairs={{0,4},{4,0},{8,12},{12,8},{1,5},{5,1},{9,13},{13,9},{2,6},{6,2},{1... | collective-permute-start | bytes 1658888 | tf_op jit(solution)/shard_map/ppermute | solution.py:23
  55.2 33.3 %collective-permute-start.2 = (bf16[72,3840]{1,0:T(8,128)(2,1)}, bf16[72,3840]{1,0:T(8,128)(2,1)}, u32[]{:S(2)}, u32[]{:S(2)}) collective-permute-start(bf16[72,3840]{1,0:T(8,128)(2,1)} %collective-permute-done.1.refs_0_), channel_id=1, source_target_pairs={{0,4},{4,0},{8,12},{12,8},{1,5},{5,1},{9,13},{13,9},{2,6},{6,2},{1... | collective-permute-start | bytes 1658888 | tf_op jit(solution)/shard_map/ppermute | solution.py:23
  99.4 14.2 %copy-start.8 = (bf16[512,64]{1,0:T(8,128)(2,1)S(1)}, bf16[512,64]{1,0:T(8,128)(2,1)}, u32[]{:S(2)}) copy-start(bf16[512,64]{1,0:T(8,128)(2,1)} %copy-done.7) | copy-start | bytes 196612
  99.4 21.8 %copy-start.23 = (f32[32]{0:T(128)S(1)}, f32[32]{0:T(128)}, u32[]{:S(2)}) copy-start(f32[32]{0:T(128)} %param.23) | copy-start | bytes 388
  99.4 22.4 %copy-start.27 = (f32[64]{0:T(128)S(1)}, f32[64]{0:T(128)}, u32[]{:S(2)}) copy-start(f32[64]{0:T(128)} %param.25) | copy-start | bytes 772
  99.4 24.6 %copy-start.24 = (bf16[128]{0:T(256)(128)(2,1)S(1)}, bf16[128]{0:T(256)(128)(2,1)}, u32[]{:S(2)}) copy-start(bf16[128]{0:T(256)(128)(2,1)} %param.28) | copy-start | bytes 772
  108.5 16.2 %copy-start.4 = (f32[4,32,128]{2,1,0:T(8,128)}, f32[4,32,128]{2,1,0:T(8,128)S(1)}, u32[]{:S(2)}) copy-start(f32[4,32,128]{2,1,0:T(8,128)S(1)} %gather_fusion) | copy-start | bytes 196612
  108.5 6.8 %collective-permute-start.9 = (f32[4,2,128]{2,1,0:T(2,128)S(1)}, f32[4,2,128]{2,1,0:T(2,128)S(1)}, u32[]{:S(2)}, u32[]{:S(2)}) collective-permute-start(f32[4,2,128]{2,1,0:T(2,128)S(1)} %get-tuple-element.62), channel_id=1, source_target_pairs={{0,1},{1,2},{2,3},{4,5},{5,6},{6,7},{8,9},{9,10},{10,11},{12,13},{... | collective-permute-start | bytes 12296 | tf_op jit(solution)/shard_map/ppermute | solution.py:23
  112.2 5.5 %collective-permute-start.10 = (f32[4,2,128]{2,1,0:T(2,128)S(1)}, f32[4,2,128]{2,1,0:T(2,128)S(1)}, u32[]{:S(2)}, u32[]{:S(2)}) collective-permute-start(f32[4,2,128]{2,1,0:T(2,128)S(1)} %get-tuple-element.61), channel_id=1, source_target_pairs={{1,0},{2,1},{3,2},{5,4},{6,5},{7,6},{9,8},{10,9},{11,10},{13,12},{... | collective-permute-start | bytes 12296 | tf_op jit(solution)/shard_map/ppermute | solution.py:23
  117.8 5.9 %collective-permute-start.11 = (f32[4,36,8]{2,1,0:T(8,128)S(1)}, f32[4,36,8]{2,1,0:T(8,128)S(1)}, u32[]{:S(2)}, u32[]{:S(2)}) collective-permute-start(f32[4,36,8]{2,1,0:T(8,128)S(1)} %get-tuple-element.38), channel_id=1, source_target_pairs={{0,4},{4,8},{8,12},{1,5},{5,9},{9,13},{2,6},{6,10},{10,14},{3,7},{... | collective-permute-start | bytes 13832 | tf_op jit(solution)/shard_map/ppermute | solution.py:23
  119.1 4.9 %collective-permute-start.12 = (f32[4,36,8]{2,1,0:T(8,128)S(1)}, f32[4,36,8]{2,1,0:T(8,128)S(1)}, u32[]{:S(2)}, u32[]{:S(2)}) collective-permute-start(f32[4,36,8]{2,1,0:T(8,128)S(1)} %get-tuple-element.37), channel_id=1, source_target_pairs={{4,0},{8,4},{12,8},{5,1},{9,5},{13,9},{6,2},{10,6},{14,10},{7,3},{... | collective-permute-start | bytes 13832 | tf_op jit(solution)/shard_map/ppermute | solution.py:23
  130.3 4.6 %collective-permute-start.15 = (f32[32,2]{1,0:T(8,128)}, f32[32,2]{1,0:T(8,128)S(1)}, u32[]{:S(2)}, u32[]{:S(2)}) collective-permute-start(f32[32,2]{1,0:T(8,128)} %get-tuple-element.21), channel_id=1, source_target_pairs={{0,3},{1,0},{2,1},{3,2},{4,7},{5,4},{6,5},{7,6},{8,11},{9,8},{10,9... | collective-permute-start | bytes 776 | tf_op jit(solution)/shard_map/ppermute | solution.py:23
  132.9 4.8 %collective-permute-start.14 = (f32[32,2]{1,0:T(8,128)}, f32[32,2]{1,0:T(8,128)S(1)}, u32[]{:S(2)}, u32[]{:S(2)}) collective-permute-start(f32[32,2]{1,0:T(8,128)} %get-tuple-element.21), channel_id=1, source_target_pairs={{0,2},{1,3},{2,0},{3,1},{4,6},{5,7},{6,4},{7,5},{8,10},{9,11},{10,... | collective-permute-start | bytes 776 | tf_op jit(solution)/shard_map/ppermute | solution.py:23
  133.4 5.7 %collective-permute-start.13 = (f32[32,2]{1,0:T(8,128)}, f32[32,2]{1,0:T(8,128)S(1)}, u32[]{:S(2)}, u32[]{:S(2)}) collective-permute-start(f32[32,2]{1,0:T(8,128)} %get-tuple-element.21), channel_id=1, source_target_pairs={{0,1},{1,2},{2,3},{3,0},{4,5},{5,6},{6,7},{7,4},{8,9},{9,10},{10,1... | collective-permute-start | bytes 776 | tf_op jit(solution)/shard_map/ppermute | solution.py:23
  139.9 4.5 %collective-permute-start.18 = (f32[2]{0:T(128)S(1)}, f32[2]{0:T(128)S(1)}, u32[]{:S(2)}, u32[]{:S(2)}) collective-permute-start(f32[2]{0:T(128)S(1)} %select_reduce_fusion), channel_id=1, source_target_pairs={{0,12},{4,0},{8,4},{12,8},{1,13},{5,1},{9,5},{13,9},{2,14},{6,2},{... | collective-permute-start | bytes 32 | tf_op jit(solution)/shard_map/ppermute | solution.py:23
  141.0 4.8 %collective-permute-start.17 = (f32[2]{0:T(128)S(1)}, f32[2]{0:T(128)S(1)}, u32[]{:S(2)}, u32[]{:S(2)}) collective-permute-start(f32[2]{0:T(128)S(1)} %select_reduce_fusion), channel_id=1, source_target_pairs={{0,8},{4,12},{8,0},{12,4},{1,9},{5,13},{9,1},{13,5},{2,10},{6,14},... | collective-permute-start | bytes 32 | tf_op jit(solution)/shard_map/ppermute | solution.py:23
  144.3 3.0 %collective-permute-start.16 = (f32[2]{0:T(128)S(1)}, f32[2]{0:T(128)S(1)}, u32[]{:S(2)}, u32[]{:S(2)}) collective-permute-start(f32[2]{0:T(128)S(1)} %select_reduce_fusion), channel_id=1, source_target_pairs={{0,4},{4,8},{8,12},{12,0},{1,5},{5,9},{9,13},{13,1},{2,6},{6,10},{... | collective-permute-start | bytes 32 | tf_op jit(solution)/shard_map/ppermute | solution.py:23
  (23 other events, 163.9 us)
